TPU v7x, 256 devices: a whole 4x4x8 slice. The times are simulated.
256 devices in a mesh: dp: 8 (over x, core), expert: 32 (over y, z).
Axes of the slice: x: 4, y: 4, z: 8, core: 2. Of those that a mesh axis runs over, the one named last changes fastest.
Arguments:
- out_grads: bfloat16 [32768, 3584], P(('dp', 'expert')), may hold values from -6 to 6
- route_probs: float32 [32768, 4], P(('dp', 'expert')), may hold values from 0.05 to 1
- expert_ids: int32 [32768, 4], P(('dp', 'expert')), may hold values from 0 to 31, all different within a row; in each aligned block of 128 rows (0 to 127, 128 to 255, ...) at most 24 rows name the same one
- saved_inputs: bfloat16 [32768, 4, 1024], P(('dp', 'expert')), may hold values from -0.59765625 to 0.59765625
- w_latent: bfloat16 [32, 3584, 1024], P('expert'), as said below
- block_exponents: int32 [32, 3584, 8], P('expert'), may hold values from -9 to -6, as said below
Outputs:
- input_grads: bfloat16 [32768, 4, 1024], P(('dp', 'expert'))
- weight_grads: float32 [32, 3584, 1024], P('expert', 'dp')
Inputs may be any that keep to these rules, and one draw needn't show every extreme that they name: `expert_ids`: each token names 4 different experts; the 128 tokens of one device name one expert in at most 24 slots, and some expert reaches 24. `block_exponents`: one exponent per 128 consecutive inputs of one output feature. w_latent * 2^(-exponent) lies within 0.45 of a whole number from -9 to 8.
All inputs are finite; a program needn't handle non-finite values.
Results may differ from a plain program's by a relative error of at most 0.012.
Values may be sent and summed in bfloat16 or wider, within the bound.
No kernel may reach another device: no remote copies, remote signals or barrier semaphores. Data moves between devices by JAX's collectives and lax.ppermute only.
A program may use at most 128 MiB of HBM per device.

v0:
```python
import jax
import jax.numpy as jnp
from jax import lax
from jax.sharding import PartitionSpec as P

BLK = 128


def dequantize(weight_one, exponent_one):
    shifts = jnp.repeat(-exponent_one, BLK, axis=1)
    powers = jnp.left_shift(jnp.ones_like(shifts), shifts).astype(jnp.float32)
    codes = weight_one.astype(jnp.float32) * powers
    levels = jnp.clip(jnp.floor(codes + 0.5), -8.0, 7.0)
    quantized = (levels / powers).astype(jnp.bfloat16)
    inside = ((codes >= -8.5) & (codes <= 7.5)).astype(jnp.float32)
    return (quantized, inside)


def local(out_grads, route_probs, expert_ids, saved_inputs, w_latent, block_exponents):
    peer_count = lax.axis_size("expert")
    tok_rows, top_count = expert_ids.shape
    feat_width = out_grads.shape[1]
    hidden = saved_inputs.shape[2]
    capacity = tok_rows * top_count * 3 // (2 * peer_count)
    slot_count = tok_rows * top_count
    row_count = peer_count * capacity
    flat_ids = expert_ids.reshape(slot_count)
    onehot = (flat_ids[:, None] == jnp.arange(peer_count, dtype=jnp.int32)[None, :]).astype(
        jnp.int32
    )
    before = jnp.cumsum(onehot, axis=0) - onehot
    position = jnp.sum(before * onehot, axis=1)
    target = flat_ids * capacity + position
    grads = (route_probs[:, :, None] * out_grads[:, None, :].astype(jnp.float32)).astype(
        jnp.bfloat16
    )
    send_grads = (
        jnp.zeros((row_count, feat_width), jnp.bfloat16)
        .at[target]
        .set(grads.reshape(slot_count, feat_width))
    )
    send_inputs = (
        jnp.zeros((row_count, hidden), jnp.bfloat16)
        .at[target]
        .set(saved_inputs.reshape(slot_count, hidden))
    )
    send_grads = send_grads.reshape(peer_count, capacity, feat_width)
    send_inputs = send_inputs.reshape(peer_count, capacity, hidden)
    quantized, inside = dequantize(w_latent[0], block_exponents[0])
    got_grads, got_inputs = (
        lax.all_to_all(send_grads, "expert", split_axis=0, concat_axis=0, tiled=True),
        lax.all_to_all(send_inputs, "expert", split_axis=0, concat_axis=0, tiled=True),
    )
    flat_grads = got_grads.reshape(row_count, feat_width)
    flat_inputs = got_inputs.reshape(row_count, hidden)
    back_rows = jnp.dot(flat_grads, quantized, preferred_element_type=jnp.float32).astype(
        jnp.bfloat16
    )
    returned = lax.all_to_all(
        back_rows.reshape(peer_count, capacity, hidden),
        "expert",
        split_axis=0,
        concat_axis=0,
        tiled=True,
    )
    input_grads = returned.reshape(row_count, hidden)[target].reshape(tok_rows, top_count, hidden)
    replica_count = lax.axis_size("dp")
    share_rows = feat_width // replica_count
    summed = lax.psum_scatter(
        lax.dot_general(
            flat_grads, flat_inputs, (((0,), (0,)), ((), ())), preferred_element_type=jnp.float32
        ).astype(jnp.bfloat16),
        "dp",
        scatter_dimension=0,
        tiled=True,
    ).astype(jnp.float32)
    replica_at = lax.axis_index("dp")
    keep_rows = lax.dynamic_slice_in_dim(inside, replica_at * share_rows, share_rows, 0)
    weight_grads = (summed * keep_rows)[None]
    return (input_grads, weight_grads)


def solution(mesh):
    placed = (
        P(("dp", "expert"), None),
        P(("dp", "expert"), None),
        P(("dp", "expert"), None),
        P(("dp", "expert"), None, None),
        P("expert", None, None),
        P("expert", None, None),
    )
    return jax.shard_map(
        local,
        mesh=mesh,
        in_specs=placed,
        out_specs=(P(("dp", "expert"), None, None), P("expert", "dp", None)),
        check_vma=False,
    )
```

profile of v0, /device:TPU:4, one launch (start us, length us, event | category | flops | bytes accessed | tf_op | source)
XLA Modules:
  0.0 305.2 jit_solution(6263518997989660646)
XLA Ops:
  7.2 0.8 broadcast_multiply_fusion
  7.9 0.8 copy.19
  8.8 0.1 eq.29
  8.9 0.1 copy.18
  9.1 0.1 mul.51
  9.2 1.2 reduce-window.6
  10.4 0.2 slice_reduce_fusion
  10.6 1.3 reshape.138
  12.1 3.8 %scatter_custom_fusion.1 = bf16[768,1024]{1,0:T(8,128)(2,1)} fusion(s32[512]{0:T(512)S(1)} %bitcast.51, bf16[512,1024]{1,0:T(8,128)(2,1)S(1)} %reshape.138, bf16[]{:T(256)} %constant.14.clone.1), kind=kCustom, calls=%fused_computation.21 | custom fusion | bytes 1572866 | tf_op jit(solution)/shard_map/scatter | solution.py:45
  15.9 11.5 %all-to-all-start.2 = ((bf16[32,24,1024]{2,1,0:T(8,128)(2,1)}), bf16[32,24,1024]{2,1,0:T(8,128)(2,1)S(1)}, u32[]{:S(2)}, u32[]{:S(2)}) async-start(bf16[32,24,1024]{2,1,0:T(8,128)(2,1)} %bitcast.9), calls=%async_computation.2 | async-start | bytes 3145728 | tf_op jit(solution)/shard_map/all_to_all | solution.py:52
  27.4 0.2 reduce-scatter.2.cloned.1.call-start
  27.6 4.0 %mul.55 = f32[128,4,3584]{2,1,0:T(4,128)} broadcast(bf16[128,3584]{1,0:T(8,128)(2,1)S(1)} %copy-done.1), dimensions={0,2} | broadcast | bytes 8257536 | tf_op jit(solution)/shard_map/mul | solution.py:34
  31.6 9.0 %mul.56 = f32[512,3584]{1,0:T(8,128)} reshape(f32[128,4,3584]{2,1,0:T(4,128)} %mul.55) | data formatting | bytes 14680064 | tf_op jit(solution)/shard_map/mul | solution.py:34
  40.6 0.1 copy.22
  40.7 0.1 mul.53
  40.8 11.3 %scatter_custom_fusion = bf16[768,3584]{1,0:T(8,128)(2,1)} fusion(s32[512]{0:T(512)S(1)} %bitcast.52, f32[512,3584]{1,0:T(8,128)} %mul.56, f32[512]{0:T(512)S(1)} %mul.53, bf16[]{:T(256)} %constant.14.clone.1), kind=kCustom, calls=%fused_computation.15 | custom fusion | flops 3670016 | bytes 12847106 | tf_op jit(solution)/shard_map/scatter | solution.py:40
  52.1 14.6 %all-to-all-done.2 = bf16[32,24,1024]{2,1,0:T(8,128)(2,1)S(1)} async-done(((bf16[32,24,1024]{2,1,0:T(8,128)(2,1)}), bf16[32,24,1024]{2,1,0:T(8,128)(2,1)S(1)}, u32[]{:S(2)}, u32[]{:S(2)}) %all-to-all-start.2) | async-done | bytes 1572896 | tf_op jit(solution)/shard_map/all_to_all | solution.py:52
  66.7 130.2 %all_to_all.15 = bf16[32,24,3584]{2,1,0:T(8,128)(2,1)S(1)} all-to-all(bf16[32,24,3584]{2,1,0:T(8,128)(2,1)} %bitcast.48), channel_id=1, replica_groups=mesh['dp'=8,'expert'=32] {'expert'}, dimensions={0} | all-to-all | bytes 11010048 | tf_op jit(solution)/shard_map/all_to_all | solution.py:51
  196.9 2.4 copy-done
  199.2 8.0 %bitcast_convert_fusion = bf16[3584,1024]{1,0:T(8,128)(2,1)} fusion(bf16[32,24,3584]{2,1,0:T(8,128)(2,1)S(1)} %all_to_all.15, bf16[32,24,1024]{2,1,0:T(8,128)(2,1)S(1)} %all-to-all-done.2), kind=kOutput, calls=%fused_computation.10 | convolution fusion | flops 5640814592 | bytes 14417920 | tf_op jit(solution)/shard_map/dot_general | solution.py:70
  207.2 0.9 copy-done.2
  208.1 0.5 copy.23
  208.7 9.4 %broadcast_in_dim.23 = f32[3584,8,128]{2,1,0:T(8,128)} broadcast(f32[3584,8]{1,0:T(8,128)S(1)} %copy.23), dimensions={0,1} | broadcast | bytes 14794752 | tf_op jit(solution)/shard_map/broadcast_in_dim | solution.py:10
  218.1 15.9 %convert_element_type.71 = f32[1,3584,1024]{2,1,0:T(8,128)} reshape(f32[3584,8,128]{2,1,0:T(8,128)} %broadcast_in_dim.23) | data formatting | bytes 29360128 | tf_op jit(solution)/shard_map/convert_element_type | solution.py:11
  234.0 13.4 %fusion.11 = bf16[768,1024]{1,0:T(8,128)(2,1)} fusion(bf16[768,3584]{1,0:T(8,128)(2,1)} %bitcast.50, f32[1,3584,1024]{2,1,0:T(8,128)} %convert_element_type.71, bf16[1,3584,1024]{2,1,0:T(8,128)(2,1)} %param.10), kind=kOutput, calls=%fused_computation.20 | convolution fusion | flops 5663621120 | bytes 29097984 | tf_op jit(solution)/shard_map/dot_general | solution.py:56
  247.4 4.4 %all-to-all-start.1 = ((bf16[32,24,1024]{2,1,0:T(8,128)(2,1)}), bf16[32,24,1024]{2,1,0:T(8,128)(2,1)S(1)}, u32[]{:S(2)}, u32[]{:S(2)}) async-start(bf16[32,24,1024]{2,1,0:T(8,128)(2,1)} %bitcast.7), calls=%async_computation.1 | async-start | bytes 3145728 | tf_op jit(solution)/shard_map/all_to_all | solution.py:59
  251.9 14.1 %copy.32 = f32[448,8,8,128]{3,1,2,0:T(8,128)} copy(f32[448,8,8,128]{3,2,1,0:T(8,128)} %bitcast.46) | data formatting | bytes 29360128
  265.9 10.2 %convert_bitcast_fusion = f32[3584,1024]{1,0:T(8,128)} fusion(bf16[1,3584,1024]{2,1,0:T(8,128)(2,1)} %param.10), kind=kLoop, calls=%fused_computation.3 | loop fusion | flops 3670016 | bytes 22020096 | tf_op jit(solution)/shard_map/convert_element_type | solution.py:12
  276.1 14.8 %all-to-all-done.1 = bf16[32,24,1024]{2,1,0:T(8,128)(2,1)S(1)} async-done(((bf16[32,24,1024]{2,1,0:T(8,128)(2,1)}), bf16[32,24,1024]{2,1,0:T(8,128)(2,1)S(1)}, u32[]{:S(2)}, u32[]{:S(2)}) %all-to-all-start.1) | async-done | bytes 1572896 | tf_op jit(solution)/shard_map/all_to_all | solution.py:59
  290.9 2.0 gather_fusion
  292.9 1.2 reshape.114
  294.2 4.2 %multiply_bitcast_fusion = f32[1,448,1024]{2,1,0:T(8,128)} fusion(bf16[448,1024]{1,0:T(8,128)(2,1)} %reduce-scatter.2.cloned.1.call-done, f32[3584,1024]{1,0:T(8,128)} %bitcast.49, s32[]{:T(128)S(6)} %select_n.16, f32[3584,1024]{1,0:T(8,128)} %convert_bitcast_fusion), kind=kLoop, calls=%fused_computation.19 | loop fusion | flops 3211264 | bytes 6422532 | tf_op jit(solution)/shard_map/broadcast_in_dim | solution.py:79
  (16 shorter events, 0.3 us)
Async XLA Ops:
  7.2 20.5 %copy-start.1 = (bf16[128,3584]{1,0:T(8,128)(2,1)S(1)}, bf16[128,3584]{1,0:T(8,128)(2,1)}, u32[]{:S(2)}) copy-start(bf16[128,3584]{1,0:T(8,128)(2,1)} %param.6) | copy-start | bytes 2752516
  15.9 50.8 %all-to-all-start.2 = ((bf16[32,24,1024]{2,1,0:T(8,128)(2,1)}), bf16[32,24,1024]{2,1,0:T(8,128)(2,1)S(1)}, u32[]{:S(2)}, u32[]{:S(2)}) async-start(bf16[32,24,1024]{2,1,0:T(8,128)(2,1)} %bitcast.9), calls=%async_computation.2 | async-start | bytes 3145728 | tf_op jit(solution)/shard_map/all_to_all | solution.py:52
  27.4 266.8 %reduce-scatter.2.cloned.1.call-start = ((), (), s32[]{:S(2)}) async-start(), calls=%async_computation.4 | async-start | bytes 8257536 | tf_op jit(solution)/shard_map/reduce_scatter | solution.py:69
  31.6 9.0 %copy-start.3 = (f32[128,4]{0,1:T(4,128)S(1)}, f32[128,4]{0,1:T(4,128)}, u32[]{:S(2)}) copy-start(f32[128,4]{0,1:T(4,128)} %param.7) | copy-start | bytes 6148
  196.9 2.4 copy-start
  207.2 0.9 copy-start.2
  247.4 43.5 %all-to-all-start.1 = ((bf16[32,24,1024]{2,1,0:T(8,128)(2,1)}), bf16[32,24,1024]{2,1,0:T(8,128)(2,1)S(1)}, u32[]{:S(2)}, u32[]{:S(2)}) async-start(bf16[32,24,1024]{2,1,0:T(8,128)(2,1)} %bitcast.7), calls=%async_computation.1 | async-start | bytes 3145728 | tf_op jit(solution)/shard_map/all_to_all | solution.py:59
Sparse Core Ops, SparseCore 0:
  207.4 43.4 reduce-scatter.1
where the time goes:
time: 306 us; the launch traced here: 305 us
  blocking collectives  130 us (42%)
  local copies, waits for them, and re-layouts  66.2 us (22%)
  waiting for transfers between devices  29.4 us (10%)
  other arithmetic  27.7 us (9%)
  matrix products  21.4 us (7%)
  starting transfers between devices  16.1 us (5%)
  between operations  14.1 us (5%)
    all_to_all x1, blocking collectives, local(): lax.all_to_all(send_grads, 'expert', split_axis=0, concat_axis=0, tiled=T...  130 us
    unnamed x11, local copies, waits for them, and re-layouts  18.2 us
    convert_element_type x2, local copies, waits for them, and re-layouts, dequantize(): powers = jnp.left_shift(jnp.ones_like(shifts), shifts).astype(jnp.float32)  16.4 us
    all_to_all x1, waiting for transfers between devices, local(): lax.all_to_all(back_rows.reshape(peer_count, capacity, hidden), 'expert',...  14.8 us
    all_to_all x1, waiting for transfers between devices, local(): lax.all_to_all(send_inputs, 'expert', split_axis=0, concat_axis=0, tiled=...  14.6 us
    dot_general x1, matrix products, local(): jnp.dot(flat_grads, quantized, preferred_element_type=jnp.float32)  13.4 us
    mul x3, local copies, waits for them, and re-layouts, local(): route_probs[:, :, None] * out_grads[:, None, :].astype(jnp.float32)  13.1 us
    all_to_all x1, starting transfers between devices, local(): lax.all_to_all(send_inputs, 'expert', split_axis=0, concat_axis=0, tiled=...  11.5 us
  transfers between devices with their start and end apart: 3, of which 2 were waited for; matrix products, arithmetic and copies ran while one was open for 30% of the time, Pallas kernels for 0%

commit v1 on v0

v1 whole, which is shorter than its diff:
```python
import jax
import jax.numpy as jnp
from jax import lax
from jax.sharding import Mesh, PartitionSpec as P

BLK = 128
CHUNKS = 4


def dequantize(weight_one, exponent_one):
    shifts = jnp.repeat(-exponent_one, BLK, axis=1)
    powers = jnp.left_shift(jnp.ones_like(shifts), shifts).astype(jnp.float32)
    codes = weight_one.astype(jnp.float32) * powers
    levels = jnp.clip(jnp.floor(codes + 0.5), -8.0, 7.0)
    return (levels / powers).astype(jnp.bfloat16)


def kept(weight_one, exponent_one):
    shifts = jnp.repeat(-exponent_one, BLK, axis=1)
    powers = jnp.left_shift(jnp.ones_like(shifts), shifts).astype(jnp.float32)
    codes = weight_one.astype(jnp.float32) * powers
    return ((codes >= -8.5) & (codes <= 7.5)).astype(jnp.float32)


def local(out_grads, route_probs, expert_ids, saved_inputs, w_latent, block_exponents):
    ny, nz = lax.axis_size("y"), lax.axis_size("z")
    experts = ny * nz
    tok, topk = expert_ids.shape
    feat = out_grads.shape[1]
    hidden = saved_inputs.shape[2]
    cap = tok * topk * 3 // (2 * experts)
    slots = tok * topk
    rows = experts * cap
    width = feat // CHUNKS
    z = lax.axis_index("z")

    gathered = [
        lax.all_gather(out_grads[:, c * width : (c + 1) * width], "z", axis=0, tiled=False)
        for c in range(CHUNKS)
    ]
    small = jnp.concatenate([route_probs, expert_ids.astype(jnp.float32)], axis=1)
    small = lax.all_gather(small.T, "z", axis=0, tiled=False)
    probs_z = small[:, :topk, :]
    ids_z = small[:, topk:, :].astype(jnp.int32)

    flat_ids = expert_ids.reshape(slots)
    onehot = flat_ids[:, None] == jnp.arange(experts, dtype=jnp.int32)[None, :]
    tri = (jnp.arange(slots)[:, None] > jnp.arange(slots)[None, :]).astype(jnp.bfloat16)
    before = jnp.dot(tri, onehot.astype(jnp.bfloat16), preferred_element_type=jnp.float32)
    position = jnp.sum(jnp.where(onehot, before, 0.0), axis=1).astype(jnp.int32)
    target = flat_ids * cap + position
    place = (jnp.arange(rows, dtype=jnp.int32)[:, None] == target[None, :]).astype(jnp.bfloat16)
    send_inputs = jnp.dot(
        place, saved_inputs.reshape(slots, hidden), preferred_element_type=jnp.float32
    ).astype(jnp.bfloat16)
    got_inputs = lax.all_to_all(
        send_inputs.reshape(experts, cap, hidden),
        ("y", "z"), split_axis=0, concat_axis=0, tiled=True,
    ).reshape(rows, hidden)

    mine = jnp.arange(ny, dtype=jnp.int32) * nz + z
    hit = ids_z[None] == mine[:, None, None, None]
    there = jnp.any(hit, axis=2)
    prob = jnp.sum(jnp.where(hit, probs_z[None], 0.0), axis=2)
    upper = (jnp.arange(tok)[:, None] < jnp.arange(tok)[None, :]).astype(jnp.bfloat16)
    order = jnp.einsum(
        "yzt,tu->yzu", there.astype(jnp.bfloat16), upper, preferred_element_type=jnp.float32
    ).astype(jnp.int32)
    chosen = there[:, :, None, :] & (order[:, :, None, :] == jnp.arange(cap)[None, None, :, None])
    slot_prob = jnp.sum(jnp.where(chosen, prob[:, :, None, :], 0.0), axis=3)
    chosen = chosen.astype(jnp.bfloat16)

    quantized = dequantize(w_latent[0], block_exponents[0])
    back = jnp.zeros((rows, hidden), jnp.float32)
    parts = []
    for c in range(CHUNKS):
        picked = jnp.einsum(
            "yzct,ztf->yzcf", chosen, gathered[c], preferred_element_type=jnp.float32
        )
        picked = (picked * slot_prob[..., None]).astype(jnp.bfloat16)
        got = lax.all_to_all(
            picked.reshape(ny, nz * cap, width), "y", split_axis=0, concat_axis=0, tiled=True
        ).reshape(rows, width)
        back = back + jnp.dot(
            got, quantized[c * width : (c + 1) * width], preferred_element_type=jnp.float32
        )
        parts.append(
            lax.dot_general(
                got, got_inputs, (((0,), (0,)), ((), ())), preferred_element_type=jnp.float32
            ).astype(jnp.bfloat16)
        )
    returned = lax.all_to_all(
        back.astype(jnp.bfloat16).reshape(experts, cap, hidden),
        ("y", "z"), split_axis=0, concat_axis=0, tiled=True,
    ).reshape(rows, hidden)
    input_grads = jnp.dot(place.T, returned, preferred_element_type=jnp.float32).astype(
        jnp.bfloat16
    )
    summed = lax.psum_scatter(
        jnp.concatenate(parts, axis=0), ("x", "core"), scatter_dimension=0, tiled=True
    ).astype(jnp.float32)
    share = feat // (lax.axis_size("x") * lax.axis_size("core"))
    at = (lax.axis_index("x") * lax.axis_size("core") + lax.axis_index("core")) * share
    keep_rows = kept(
        lax.dynamic_slice_in_dim(w_latent[0], at, share, 0),
        lax.dynamic_slice_in_dim(block_exponents[0], at, share, 0),
    )
    return (input_grads.reshape(tok, topk, hidden), (summed * keep_rows)[None])


def solution(mesh):
    split = Mesh(mesh.devices.reshape(4, 2, 4, 8), ("x", "core", "y", "z"))
    every = ("x", "core", "y", "z")
    placed = (
        P(every, None),
        P(every, None),
        P(every, None),
        P(every, None, None),
        P(("y", "z"), None, None),
        P(("y", "z"), None, None),
    )
    return jax.shard_map(
        local,
        mesh=split,
        in_specs=placed,
        out_specs=(P(every, None, None), P(("y", "z"), ("x", "core"), None)),
        check_vma=False,
    )
```

time: 306 us -> 311 us (1.016)
  waiting for transfers between devices: 29.4 us -> 124 us
  blocking collectives: 130 us -> 70.3 us
  local copies, waits for them, and re-layouts: 66.2 us -> 19.3 us
  starting transfers between devices: 16.1 us -> 34 us
  other arithmetic: 27.7 us -> 14.1 us
  matrix products: 21.4 us -> 34.5 us
    all_to_all x1 -> x0, blocking collectives: 130 us -> none  [local(): lax.all_to_all(send_grads, 'expert', split_axis=0, concat_axis=0, tiled=T...]
    all_gather x0 -> x4, waiting for transfers between devices: none -> 82.6 us  [local(): lax.all_gather(out_grads[:, c * width:(c + 1) * width], 'z', axis=0, tile...]
    all_gather x0 -> x1, blocking collectives: none -> 70.3 us  [local(): small = lax.all_gather(small.T, 'z', axis=0, tiled=False)]
    all_to_all x2 -> x6, starting transfers between devices: 15.9 us -> 33.8 us  [the longest x4 17.2 us: local(): lax.all_to_all(picked.reshape(ny, nz * cap, width), 'y', split_axis=0, co...]
    unnamed x11 -> x37, local copies, waits for them, and re-layouts: 18.2 us -> 2.75 us
    convert_element_type x2 -> x1, local copies, waits for them, and re-layouts: 16.4 us -> 1.77 us  [dequantize(): powers = jnp.left_shift(jnp.ones_like(shifts), shifts).astype(jnp.float32)]
    mul x5 -> x0, local copies, waits for them, and re-layouts: 13.3 us -> none  [the longest x3 13.1 us: local(): route_probs[:, :, None] * out_grads[:, None, :].astype(jnp.float32)]
    dot_general x2 -> x16, matrix products: 21.4 us -> 34.5 us  [the longest x4 12.9 us: local(): lax.dot_general(got, got_inputs, (((0,), (0,)), ((), ())), preferred_elem...]
  transfers between devices with their start and end apart: 3 -> 11, of which waited for: 2 -> 5; matrix products, arithmetic and copies ran while one was open for 30% -> 17% of each run, Pallas kernels for 0% -> 0%
where the time goes in v1:
time: 311 us; the launch traced here: 310 us
  waiting for transfers between devices  124 us (40%)
  blocking collectives  70.3 us (23%)
  matrix products  34.5 us (11%)
  starting transfers between devices  34 us (11%)
  local copies, waits for them, and re-layouts  19.3 us (6%)
  between operations  14.2 us (5%)
  other arithmetic  14.1 us (5%)
    all_gather x4, waiting for transfers between devices, local(): lax.all_gather(out_grads[:, c * width:(c + 1) * width], 'z', axis=0, tile...  82.6 us
    all_gather x1, blocking collectives, local(): small = lax.all_gather(small.T, 'z', axis=0, tiled=False)  70.3 us
    all_to_all x1, waiting for transfers between devices, local(): lax.all_to_all(back.astype(jnp.bfloat16).reshape(experts, cap, hidden), (...  34.2 us
    all_to_all x4, starting transfers between devices, local(): lax.all_to_all(picked.reshape(ny, nz * cap, width), 'y', split_axis=0, co...  17.2 us
    dot_general x4, matrix products, local(): lax.dot_general(got, got_inputs, (((0,), (0,)), ((), ())), preferred_elem...  12.9 us
    all_to_all x1, starting transfers between devices, local(): lax.all_to_all(send_inputs.reshape(experts, cap, hidden), ('y', 'z'), spl...  11.6 us
    dot_general x4, matrix products, local(): jnp.dot(got, quantized[c * width:(c + 1) * width], preferred_element_type...  9.86 us
    dot_general x4, matrix products, local(): jnp.einsum('yzct,ztf->yzcf', chosen, gathered[c], preferred_element_type=...  8.12 us
  transfers between devices with their start and end apart: 11, of which 5 were waited for; matrix products, arithmetic and copies ran while one was open for 17% of the time, Pallas kernels for 0%

profile of v1, /device:TPU:4, one launch (start us, length us, event | category | flops | bytes accessed | tf_op | source)
XLA Modules:
  0.0 310.4 jit_solution(598911200673936951)
XLA Ops:
  7.2 2.3 fusion.40
  11.9 2.1 convolution_convert_fusion.4
  14.0 11.6 %all-to-all-start.5 = ((bf16[32,24,1024]{2,1,0:T(8,128)(2,1)}), bf16[32,24,1024]{2,1,0:T(8,128)(2,1)S(1)}, u32[]{:S(2)}, u32[]{:S(2)}) async-start(bf16[32,24,1024]{2,1,0:T(8,128)(2,1)} %bitcast.33), calls=%async_computation.5 | async-start | bytes 3145728 | tf_op jit(solution)/shard_map/all_to_all | solution.py:56
  26.2 70.3 %all-gather = f32[64,128]{1,0:T(8,128)S(1)} all-gather(f32[8,128]{1,0:T(8,128)S(1)} %maximum_bitcast_fusion), channel_id=2, replica_groups=mesh['x'=4,'core'=2,'y'=4,'z'=8] {'z'}, dimensions={0}, use_global_device_ids=true | all-gather | bytes 36864 | tf_op jit(solution)/shard_map/all_gather | solution.py:42
  97.1 2.0 fusion.5
  99.2 1.3 copy.52
  100.5 4.3 %all-to-all-start.2 = ((bf16[4,192,896]{2,1,0:T(8,128)(2,1)}), bf16[4,192,896]{2,1,0:T(8,128)(2,1)S(1)}, u32[]{:S(2)}, u32[]{:S(2)}) async-start(bf16[4,192,896]{2,1,0:T(8,128)(2,1)} %bitcast.21), calls=%async_computation.2 | async-start | bytes 2752512 | tf_op jit(solution)/shard_map/all_to_all | solution.py:81
  104.8 16.7 %all-gather.12.cloned.1.call-done = bf16[1024,896]{1,0:T(8,128)(2,1)} async-done(((bf16[128,896]{1,0:T(8,128)(2,1)}), bf16[1024,896]{1,0:T(8,128)(2,1)}) %all-gather.12.cloned.1.call-update) | async-done | bytes 1835024 | tf_op jit(solution)/shard_map/all_gather | solution.py:38
  121.5 2.0 fusion.6
  124.7 4.3 %all-to-all-start.1 = ((bf16[4,192,896]{2,1,0:T(8,128)(2,1)}), bf16[4,192,896]{2,1,0:T(8,128)(2,1)S(1)}, u32[]{:S(2)}, u32[]{:S(2)}) async-start(bf16[4,192,896]{2,1,0:T(8,128)(2,1)} %bitcast.15), calls=%async_computation.1 | async-start | bytes 2752512 | tf_op jit(solution)/shard_map/all_to_all | solution.py:81
  129.0 33.8 %all-gather.10.cloned.1.call-done = bf16[1024,896]{1,0:T(8,128)(2,1)} async-done(((bf16[128,896]{1,0:T(8,128)(2,1)}), bf16[1024,896]{1,0:T(8,128)(2,1)}) %all-gather.10.cloned.1.call-update) | async-done | bytes 1835024 | tf_op jit(solution)/shard_map/all_gather | solution.py:38
  162.9 2.0 fusion.7
  167.2 4.3 %all-to-all-start = ((bf16[4,192,896]{2,1,0:T(8,128)(2,1)}), bf16[4,192,896]{2,1,0:T(8,128)(2,1)S(1)}, u32[]{:S(2)}, u32[]{:S(2)}) async-start(bf16[4,192,896]{2,1,0:T(8,128)(2,1)} %bitcast.7), calls=%async_computation | async-start | bytes 2752512 | tf_op jit(solution)/shard_map/all_to_all | solution.py:81
  171.5 32.0 %all-gather.16.cloned.1.call-done = bf16[1024,896]{1,0:T(8,128)(2,1)} async-done(((bf16[128,896]{1,0:T(8,128)(2,1)}), bf16[1024,896]{1,0:T(8,128)(2,1)}) %all-gather.16.cloned.1.call-update) | async-done | bytes 1835024 | tf_op jit(solution)/shard_map/all_gather | solution.py:38
  203.5 2.0 fusion.4
  206.8 4.3 %all-to-all-start.3 = ((bf16[4,192,896]{2,1,0:T(8,128)(2,1)}), bf16[4,192,896]{2,1,0:T(8,128)(2,1)}, u32[]{:S(2)}, u32[]{:S(2)}) async-start(bf16[4,192,896]{2,1,0:T(8,128)(2,1)} %bitcast.27), calls=%async_computation.3 | async-start | bytes 2752512 | tf_op jit(solution)/shard_map/all_to_all | solution.py:81
  211.2 3.6 %convolution_convert_fusion.1 = bf16[896,1024]{1,0:T(8,128)(2,1)S(1)} fusion(bf16[768,896]{1,0:T(8,128)(2,1)} %bitcast.119, bf16[768,1024]{1,0:T(8,128)(2,1)} %bitcast.114), kind=kOutput, calls=%fused_computation.27 | convolution fusion | flops 1410203648 | bytes 4784128 | tf_op jit(solution)/shard_map/dot_general | solution.py:88
  214.8 2.9 convolution_convert_fusion.2
  217.6 2.9 convolution_convert_fusion.3
  220.5 5.3 %all-to-all-done.3 = bf16[4,192,896]{2,1,0:T(8,128)(2,1)} async-done(((bf16[4,192,896]{2,1,0:T(8,128)(2,1)}), bf16[4,192,896]{2,1,0:T(8,128)(2,1)}, u32[]{:S(2)}, u32[]{:S(2)}) %all-to-all-start.3) | async-done | bytes 1376288 | tf_op jit(solution)/shard_map/all_to_all | solution.py:81
  225.9 3.6 %convolution_convert_fusion = bf16[896,1024]{1,0:T(8,128)(2,1)S(1)} fusion(bf16[768,896]{1,0:T(8,128)(2,1)} %bitcast.28, bf16[768,1024]{1,0:T(8,128)(2,1)} %bitcast.115), kind=kOutput, calls=%fused_computation.26 | convolution fusion | flops 1410203648 | bytes 4784128 | tf_op jit(solution)/shard_map/dot_general | solution.py:88
  229.5 3.9 %pad_maximum_fusion = bf16[3584,1024]{1,0:T(8,128)(2,1)} fusion(bf16[896,1024]{1,0:T(8,128)(2,1)S(1)} %convolution_convert_fusion, bf16[896,1024]{1,0:T(8,128)(2,1)S(1)} %convolution_convert_fusion.1, bf16[896,1024]{1,0:T(8,128)(2,1)S(1)} %copy-done.2, bf16[896,1024]{1,0:T(8,128)(2,1)S(1)} %copy-done.3), kind=kLoop, calls=%fused_computation.6 | loop fusion | flops 29360128 | bytes 14680064 | tf_op jit(solution)/shard_map/concatenate | solution.py:100
  234.3 1.8 copy.50
  236.1 5.2 %broadcast_in_dim.67 = f32[3584,8,128]{2,1,0:T(8,128)S(1)} broadcast(f32[3584,8]{1,0:T(8,128)} %copy.50), dimensions={0,1} | broadcast | bytes 14794752 | tf_op jit(solution)/shard_map/broadcast_in_dim | solution.py:11
  241.4 6.5 %fusion.3 = bf16[3584,1024]{1,0:T(8,128)(2,1)S(1)} fusion(f32[448,8,8,128]{3,2,1,0:T(8,128)S(1)} %bitcast.104, bf16[1,3584,1024]{2,1,0:T(8,128)(2,1)S(1)} %bitcast.106), kind=kLoop, calls=%fused_computation.5 | loop fusion | flops 25690112 | bytes 29360128 | tf_op jit(solution)/shard_map/convert_element_type | solution.py:15
  247.9 1.8 fusion.10
  249.8 1.8 fusion.12
  251.6 3.3 %fusion.8 = f32[768,1024]{1,0:T(8,128)S(1)} fusion(bf16[768,896]{1,0:T(8,128)(2,1)} %bitcast.28, bf16[3584,1024]{1,0:T(8,128)(2,1)S(1)} %fusion.3), kind=kOutput, calls=%fused_computation.17 | convolution fusion | flops 1409286144 | bytes 6356992 | tf_op jit(solution)/shard_map/dot_general | solution.py:84
  254.9 3.0 add_convert_fusion
  257.8 5.0 %all-to-all-start.4 = ((bf16[32,24,1024]{2,1,0:T(8,128)(2,1)}), bf16[32,24,1024]{2,1,0:T(8,128)(2,1)S(1)}, u32[]{:S(2)}, u32[]{:S(2)}) async-start(bf16[32,24,1024]{2,1,0:T(8,128)(2,1)} %bitcast.29), calls=%async_computation.4 | async-start | bytes 3145728 | tf_op jit(solution)/shard_map/all_to_all | solution.py:92
  263.0 34.2 %all-to-all-done.4 = bf16[32,24,1024]{2,1,0:T(8,128)(2,1)S(1)} async-done(((bf16[32,24,1024]{2,1,0:T(8,128)(2,1)}), bf16[32,24,1024]{2,1,0:T(8,128)(2,1)S(1)}, u32[]{:S(2)}, u32[]{:S(2)}) %all-to-all-start.4) | async-done | bytes 1572896 | tf_op jit(solution)/shard_map/all_to_all | solution.py:92
  300.7 3.2 %select_bitcast_fusion = f32[1,448,1024]{2,1,0:T(8,128)} fusion(bf16[448,1024]{1,0:T(8,128)(2,1)S(1)} %copy-done.12, f32[56,8,8,128]{3,2,1,0:T(8,128)S(1)} %bitcast.107, bf16[1,3584,1024]{2,1,0:T(8,128)(2,1)} %param.10, s32[]{:T(128)S(6)} %select_n.19), kind=kLoop, calls=%fused_computation.25 | loop fusion | flops 3211264 | bytes 5505028 | tf_op jit(solution)/shard_map/broadcast_in_dim | solution.py:108
  (80 shorter events, 12.7 us)
Async XLA Ops:
  7.2 3.9 %copy-start.14 = (s32[128,4]{0,1:T(4,128)S(1)}, s32[128,4]{0,1:T(4,128)}, u32[]{:S(2)}) copy-start(s32[128,4]{0,1:T(4,128)} %param.8) | copy-start | bytes 6148
  7.2 4.1 %copy-start.11 = (bf16[128,4,1024]{2,1,0:T(4,128)(2,1)S(1)}, bf16[128,4,1024]{2,1,0:T(4,128)(2,1)}, u32[]{:S(2)}) copy-start(bf16[128,4,1024]{2,1,0:T(4,128)(2,1)} %param.9) | copy-start | bytes 3145732
  7.2 90.0 %all-gather.14.cloned.1.call-start = ((), (), s32[]{:S(2)}) async-start(), calls=%async_computation.10 | async-start | bytes 2064384 | tf_op jit(solution)/shard_map/all_gather | solution.py:38
  9.5 112.0 %all-gather.12.cloned.1.call-start = ((), (), s32[]{:S(2)}) async-start(), calls=%async_computation.9 | async-start | bytes 2064384 | tf_op jit(solution)/shard_map/all_gather | solution.py:38
  10.3 152.6 %all-gather.10.cloned.1.call-start = ((), (), s32[]{:S(2)}) async-start(), calls=%async_computation.8 | async-start | bytes 2064384 | tf_op jit(solution)/shard_map/all_gather | solution.py:38
  14.0 12.2 %copy-start.15 = (f32[128,4]{0,1:T(4,128)S(1)}, f32[128,4]{0,1:T(4,128)}, u32[]{:S(2)}) copy-start(f32[128,4]{0,1:T(4,128)} %param.7) | copy-start | bytes 6148
  14.0 86.5 %all-to-all-start.5 = ((bf16[32,24,1024]{2,1,0:T(8,128)(2,1)}), bf16[32,24,1024]{2,1,0:T(8,128)(2,1)S(1)}, u32[]{:S(2)}, u32[]{:S(2)}) async-start(bf16[32,24,1024]{2,1,0:T(8,128)(2,1)} %bitcast.33), calls=%async_computation.5 | async-start | bytes 3145728 | tf_op jit(solution)/shard_map/all_to_all | solution.py:56
  25.6 177.9 %all-gather.16.cloned.1.call-start = ((), (), s32[]{:S(2)}) async-start(), calls=%async_computation.11 | async-start | bytes 2064384 | tf_op jit(solution)/shard_map/all_gather | solution.py:38
  100.5 23.0 %copy-start.4 = (bf16[32,24,1024]{2,1,0:T(8,128)(2,1)}, bf16[32,24,1024]{2,1,0:T(8,128)(2,1)S(1)}, u32[]{:S(2)}) copy-start(bf16[32,24,1024]{2,1,0:T(8,128)(2,1)S(1)} %all-to-all-done.5) | copy-start | bytes 4718596
  100.5 24.2 %all-to-all-start.2 = ((bf16[4,192,896]{2,1,0:T(8,128)(2,1)}), bf16[4,192,896]{2,1,0:T(8,128)(2,1)S(1)}, u32[]{:S(2)}, u32[]{:S(2)}) async-start(bf16[4,192,896]{2,1,0:T(8,128)(2,1)} %bitcast.21), calls=%async_computation.2 | async-start | bytes 2752512 | tf_op jit(solution)/shard_map/all_to_all | solution.py:81
  124.7 40.1 %copy-start.6 = (bf16[4,192,896]{2,1,0:T(8,128)(2,1)}, bf16[4,192,896]{2,1,0:T(8,128)(2,1)S(1)}, u32[]{:S(2)}) copy-start(bf16[4,192,896]{2,1,0:T(8,128)(2,1)S(1)} %all-to-all-done.2) | copy-start | bytes 4128772
  124.7 41.4 %all-to-all-start.1 = ((bf16[4,192,896]{2,1,0:T(8,128)(2,1)}), bf16[4,192,896]{2,1,0:T(8,128)(2,1)S(1)}, u32[]{:S(2)}, u32[]{:S(2)}) async-start(bf16[4,192,896]{2,1,0:T(8,128)(2,1)} %bitcast.15), calls=%async_computation.1 | async-start | bytes 2752512 | tf_op jit(solution)/shard_map/all_to_all | solution.py:81
  166.1 1.1 copy-start.8
  167.2 39.6 %all-to-all-start = ((bf16[4,192,896]{2,1,0:T(8,128)(2,1)}), bf16[4,192,896]{2,1,0:T(8,128)(2,1)S(1)}, u32[]{:S(2)}, u32[]{:S(2)}) async-start(bf16[4,192,896]{2,1,0:T(8,128)(2,1)} %bitcast.7), calls=%async_computation | async-start | bytes 2752512 | tf_op jit(solution)/shard_map/all_to_all | solution.py:81
  206.8 10.9 %copy-start = (bf16[4,192,896]{2,1,0:T(8,128)(2,1)}, bf16[4,192,896]{2,1,0:T(8,128)(2,1)S(1)}, u32[]{:S(2)}) copy-start(bf16[4,192,896]{2,1,0:T(8,128)(2,1)S(1)} %all-to-all-done) | copy-start | bytes 4128772
  206.8 19.1 %all-to-all-start.3 = ((bf16[4,192,896]{2,1,0:T(8,128)(2,1)}), bf16[4,192,896]{2,1,0:T(8,128)(2,1)}, u32[]{:S(2)}, u32[]{:S(2)}) async-start(bf16[4,192,896]{2,1,0:T(8,128)(2,1)} %bitcast.27), calls=%async_computation.3 | async-start | bytes 2752512 | tf_op jit(solution)/shard_map/all_to_all | solution.py:81
  211.1 88.4 %reduce-scatter.2.cloned.1.call-start = ((), (), s32[]{:S(2)}) async-start(), calls=%async_computation.7 | async-start | bytes 8257536 | tf_op jit(solution)/shard_map/reduce_scatter | solution.py:99
  211.1 3.6 %copy-start.5 = (bf16[32,24,1024]{2,1,0:T(8,128)(2,1)S(1)}, bf16[32,24,1024]{2,1,0:T(8,128)(2,1)}, u32[]{:S(2)}) copy-start(bf16[32,24,1024]{2,1,0:T(8,128)(2,1)} %copy-done.4) | copy-start | bytes 4718596
  211.1 3.6 %copy-start.9 = (bf16[4,192,896]{2,1,0:T(8,128)(2,1)S(1)}, bf16[4,192,896]{2,1,0:T(8,128)(2,1)}, u32[]{:S(2)}) copy-start(bf16[4,192,896]{2,1,0:T(8,128)(2,1)} %copy-done.8) | copy-start | bytes 4128772
  225.9 3.6 %copy-start.2 = (bf16[896,1024]{1,0:T(8,128)(2,1)S(1)}, bf16[896,1024]{1,0:T(8,128)(2,1)}, u32[]{:S(2)}) copy-start(bf16[896,1024]{1,0:T(8,128)(2,1)} %convolution_convert_fusion.2) | copy-start | bytes 5505028
  225.9 3.6 %copy-start.3 = (bf16[896,1024]{1,0:T(8,128)(2,1)S(1)}, bf16[896,1024]{1,0:T(8,128)(2,1)}, u32[]{:S(2)}) copy-start(bf16[896,1024]{1,0:T(8,128)(2,1)} %convolution_convert_fusion.3) | copy-start | bytes 5505028
  233.4 0.9 copy-start.13
  234.3 7.0 %slice-start = ((s8[7340032]{0:T(1024)(128)(4,1)}), s8[3145728]{0:T(1024)(128)(4,1)S(1)}, s32[]{:S(2)}) async-start(s8[7340032]{0:T(1024)(128)(4,1)} %bitcast.105), calls=%async_computation.12 | async-start | bytes 6291456
  236.1 5.3 %slice-start.1 = ((s8[7340032]{0:T(1024)(128)(4,1)}), s8[4194304]{0:T(1024)(128)(4,1)S(1)}, s32[]{:S(2)}) async-start(s8[7340032]{0:T(1024)(128)(4,1)} %bitcast.105), calls=%async_computation.13 | async-start | bytes 8388608
  241.4 6.5 %copy-start.7 = (bf16[4,192,896]{2,1,0:T(8,128)(2,1)S(1)}, bf16[4,192,896]{2,1,0:T(8,128)(2,1)}, u32[]{:S(2)}) copy-start(bf16[4,192,896]{2,1,0:T(8,128)(2,1)} %copy-done.6) | copy-start | bytes 4128772
  247.9 1.8 copy-start.10
  251.6 3.3 %copy-start.1 = (bf16[4,192,896]{2,1,0:T(8,128)(2,1)S(1)}, bf16[4,192,896]{2,1,0:T(8,128)(2,1)}, u32[]{:S(2)}) copy-start(bf16[4,192,896]{2,1,0:T(8,128)(2,1)} %copy-done) | copy-start | bytes 4128772
  257.8 39.4 %all-to-all-start.4 = ((bf16[32,24,1024]{2,1,0:T(8,128)(2,1)}), bf16[32,24,1024]{2,1,0:T(8,128)(2,1)S(1)}, u32[]{:S(2)}, u32[]{:S(2)}) async-start(bf16[32,24,1024]{2,1,0:T(8,128)(2,1)} %bitcast.29), calls=%async_computation.4 | async-start | bytes 3145728 | tf_op jit(solution)/shard_map/all_to_all | solution.py:92
  299.5 1.2 copy-start.12
Sparse Core Ops, SparseCore 0:
  9.8 69.2 all-gather.13
  80.9 40.5 all-gather.11
  123.9 38.9 all-gather.9
  164.5 38.9 all-gather.15
  233.6 44.3 reduce-scatter.1
